TPU v7x, 32 devices: a whole 2x2x4 slice. The times are simulated.
32 devices in a mesh: grp: 2 (over y), row: 8 (over z, x), col: 2 (over core).
Axes of the slice: x: 2, y: 2, z: 4, core: 2. Of those that a mesh axis runs over, the one named last changes fastest.
Arguments:
- queries: bfloat16 [2048, 1536], P(('grp', 'row', 'col')), parts along dimension 0, may hold values from -24 to 24
- key_rows: bfloat16 [2048, 1536], P(('grp', 'row', 'col')), parts along dimension 0, may hold values from -8 to 8
- value_rows: bfloat16 [2048, 1536], P(('grp', 'row', 'col')), parts along dimension 0, may hold values from -6 to 6
- latent: float32 [2048, 128], P(('grp', 'row', 'col')), parts along dimension 0, may hold values from -6 to 6
- out_proj: bfloat16 [1536, 128], replicated, may hold values from -0.625 to 0.625
- tile_owner: int32 [512, 1], P(('grp', 'row', 'col')), parts along dimension 0, may hold values from 0 to 7; in each aligned block of 16 rows (0 to 15, 16 to 31, ...) at most 4 rows name the same one
- tile_count: int32 [512], P(('grp', 'row', 'col')), parts along dimension 0, may hold values from 3 to 4
- window_reach: int32 [2, 3], replicated, may hold values from 0 to 3
- refine_query: bfloat16 [128, 128], replicated, may hold values from -0.5 to 0.5
- refine_key: bfloat16 [128, 128], replicated, may hold values from -0.5 to 0.5
- refine_value: bfloat16 [128, 128], replicated, may hold values from -0.5 to 0.5
- refine_out: bfloat16 [128, 128], replicated, may hold values from -0.5 to 0.5
Outputs:
- updated: float32 [2048, 128], P(('grp', 'row', 'col')), parts along dimension 0
- refined: float32 [2048, 128], P(('grp', 'row', 'col')), parts along dimension 0
There are 2 independent parts, one for each index of `grp`. A program takes and returns all parts, laid end to end along the dimension named above; an argument that names none is the same for every part. Nothing has to cross between parts.
Inputs may be any that keep to these rules, and one draw needn't show every extreme that they name: `tile_owner`: among the 16 tiles of one device no owner is named by more than 4 tiles, and some device reaches 4 for some owner.
All inputs are finite; a program needn't handle non-finite values.
Results may differ from a plain program's by a relative error of at most 0.024.
Values may be sent and summed in bfloat16 or wider, within the bound.
A program may use at most 128 MiB of HBM per device.

v0:
```python
import functools
import math

import jax
import jax.numpy as jnp
import numpy as np
from jax import lax
from jax.experimental import pallas as pl
from jax.experimental.pallas import tpu as pltpu
from jax.sharding import PartitionSpec as P

HEAD = 128
LAT = 128
RHEADS = 2
TILE = 4
GW = 64
GH = 64
MAX_REACH = 3
MESH = pl.DeviceIdType.MESH
NEG = -1e30


def near_rows(rows, cols, tok):
    spots = {}
    for r in range(rows):
        for c in range(cols):
            p = (r * cols + c) * tok + np.arange(tok)
            spots[r, c] = np.unique(np.stack([p // (GH * GW), p // GW % GH], 1), axis=0)
    found = []
    for d in sorted(range(1 - rows, rows), key=abs):
        if d == 0:
            continue
        hit = False
        for r in range(max(0, -d), min(rows, rows - d)):
            for c in range(cols):
                gap = np.abs(spots[r, c][:, None] - spots[r + d, c][None])
                hit = hit or bool((gap.max(-1) <= MAX_REACH).any())
        if hit:
            found.append(d)
    return found


def kernel(
    dims, near,
    q_hbm, k_hbm, v_hbm, lat_hbm, wo_hbm, owner_ref, count_ref, reach_ref,
    rq_hbm, rk_hbm, rv_hbm, ro_hbm,
    upd_ref, ref_ref,
    qb, kb, vb, wo, lat, rw, ro, acc, part_out, part_in, nb, code, bias,
    z_send, z_recv, s_send, s_recv, c_send, c_recv, p_send, p_recv,
    n_send, n_recv, m_send, m_recv, own_sem, w_sem,
):
    G, S, C, hg, T = dims
    R = G * S
    grp = lax.axis_index("grp")
    row = lax.axis_index("row")
    col = lax.axis_index("col")
    g = row // S
    s = row % S
    n_near = len(near)
    tiles = T // TILE

    def head_cols(group, h):
        return pl.ds(pl.multiple_of((group * hg + h) * HEAD, HEAD), HEAD)

    arrays = ((q_hbm, qb), (k_hbm, kb), (v_hbm, vb))

    def slot(a, h, group):
        return qb.at[h, group] if a == 0 else arrays[a][1].at[h, s, col, group]

    own = [
        [
            pltpu.make_async_copy(
                arrays[a][0].at[:, head_cols(g, h)], slot(a, h, g), own_sem.at[h, a]
            )
            for a in range(3)
        ]
        for h in range(hg)
    ]
    depth = hg * HEAD
    weights = [
        pltpu.make_async_copy(
            wo_hbm.at[pl.ds(pl.multiple_of(g * depth, depth), depth)], wo, w_sem.at[0]
        ),
        pltpu.make_async_copy(lat_hbm, lat, w_sem.at[1]),
        pltpu.make_async_copy(rq_hbm, rw.at[0], w_sem.at[2]),
        pltpu.make_async_copy(rk_hbm, rw.at[1], w_sem.at[3]),
        pltpu.make_async_copy(rv_hbm, rw.at[2], w_sem.at[4]),
        pltpu.make_async_copy(ro_hbm, ro, w_sem.at[5]),
    ]

    barrier = pltpu.get_barrier_semaphore()
    greeted = (
        [(lax.rem(g + d, G) * S + s, col) for d in range(1, G)]
        + [(g * S + lax.rem(s + d, S), col) for d in range(1, S)]
        + [(row, lax.rem(col + d, C)) for d in range(1, C)]
    )
    for r2, c2 in greeted:
        pl.semaphore_signal(barrier, inc=1, device_id=(grp, r2, c2), device_id_type=MESH)

    for d in near:
        @pl.when((row + d >= 0) & (row + d < R))
        def _():
            pl.semaphore_signal(
                barrier, inc=1, device_id=(grp, row + d, col), device_id_type=MESH
            )

    for h in range(hg):
        for a in range(3):
            own[h][a].start()
    for w in weights:
        w.start()

    lane = lax.broadcasted_iota(jnp.int32, (8, 128), 1)
    sub = lax.broadcasted_iota(jnp.int32, (T, 1), 0)
    code_row = jnp.full((8, 128), -1, jnp.int32)
    owner_col = jnp.zeros((T, 1), jnp.int32)
    live_col = jnp.zeros((T, 1), jnp.int32)
    for t in range(tiles):
        own_t, cnt_t = owner_ref[t], count_ref[t]
        code_row = jnp.where(
            (lane // TILE == t) & (lane % TILE < cnt_t) & (lane < T), own_t, code_row
        )
        owner_col = jnp.where(sub // TILE == t, own_t, owner_col)
        live_col = jnp.where((sub // TILE == t) & (sub % TILE < cnt_t), 1, live_col)
    code[0] = code_row.astype(jnp.float32)

    def near_ok(d):
        return (row - d >= 0) & (row - d < R)

    def goes(d):
        return (row + d >= 0) & (row + d < R)

    for i, d in enumerate(near):
        @pl.when(jnp.logical_not(near_ok(d)))
        def _():
            nb[i + 1] = jnp.zeros((T, LAT), jnp.bfloat16)
            code[i + 1] = jnp.full((8, 128), -1.0, jnp.float32)

    pl.semaphore_wait(
        barrier, len(greeted) + sum([near_ok(d).astype(jnp.int32) for d in near])
    )

    def z_copy(h, a, d):
        to = lax.rem(g + d, G)
        return pltpu.make_async_remote_copy(
            src_ref=arrays[a][0].at[:, head_cols(to, h)],
            dst_ref=slot(a, h, g),
            send_sem=z_send.at[h, a, d - 1],
            recv_sem=z_recv.at[h, a, d - 1],
            device_id=(grp, to * S + s, col),
            device_id_type=MESH,
        )

    z_copies = {}
    for h, a in [(h, a) for a in (1, 2, 0) for h in range(hg)]:
        for d in list(range(2, G)) + [1]:
            z_copies[h, a, d] = z_copy(h, a, d)
            z_copies[h, a, d].start()

    def m_copy(i, d):
        return pltpu.make_async_remote_copy(
            src_ref=code.at[0],
            dst_ref=code.at[i + 1],
            send_sem=m_send.at[i],
            recv_sem=m_recv.at[i],
            device_id=(grp, row + d, col),
            device_id_type=MESH,
        )

    for i, d in enumerate(near):
        @pl.when(goes(d))
        def _():
            m_copy(i, d).start()

    s_copies, c_copies = {}, {}

    def c_forward(h, a, j):
        buf = arrays[a][1]
        src = lax.rem(s - j + S, S)
        for d in range(1, C):
            c_copies[h, a, j, d] = pltpu.make_async_remote_copy(
                src_ref=buf.at[h, src, col],
                dst_ref=buf.at[h, src, col],
                send_sem=c_send.at[h, a - 1, j, d - 1],
                recv_sem=c_recv.at[h, a - 1, j, d - 1],
                device_id=(grp, row, lax.rem(col + d, C)),
                device_id_type=MESH,
            )
            c_copies[h, a, j, d].start()

    def s_forward(h, a, e):
        buf = arrays[a][1]
        block = buf.at[h, s, col, lax.rem(g - e + G, G)]
        for d in range(1, S):
            s_copies[h, a, e, d] = pltpu.make_async_remote_copy(
                src_ref=block,
                dst_ref=block,
                send_sem=s_send.at[h, a - 1, e, d - 1],
                recv_sem=s_recv.at[h, a - 1, e, d - 1],
                device_id=(grp, g * S + lax.rem(s + d, S), col),
                device_id_type=MESH,
            )
            s_copies[h, a, e, d].start()

    def spread(h, kinds=(1, 2)):
        for a in kinds:
            for e in range(1, G):
                z_copies[h, a, e].wait_recv()
                s_forward(h, a, e)
            c_forward(h, a, 0)

    def pass_on(h, kinds=(1, 2)):
        for a in kinds:
            for d in range(1, S):
                for e in range(G):
                    s_copies[h, a, e, d].wait_recv()
                c_forward(h, a, d)

    keys = S * C * G * T
    fold = math.log2(math.e) / math.sqrt(HEAD)

    def soften(h):
        query = qb[h].reshape(G * T, HEAD)
        key = kb[h].reshape(keys, HEAD)
        scores = lax.dot_general(
            query, key, (((1,), (1,)), ((), ())), preferred_element_type=jnp.float32
        )
        largest = jnp.max(scores, axis=1, keepdims=True)
        terms = jnp.exp2((scores - largest) * fold)
        return terms.astype(jnp.bfloat16), jnp.sum(terms, axis=1, keepdims=True)

    def blend(h, terms, total):
        value = vb[h].reshape(keys, HEAD)
        mixed = jnp.dot(terms, value, preferred_element_type=jnp.float32)
        attended = (mixed / total).astype(jnp.bfloat16)
        share = jnp.dot(
            attended, wo[h * HEAD : (h + 1) * HEAD], preferred_element_type=jnp.float32
        ).reshape(G, T, LAT)
        return share if h == 0 else acc[...] + share

    def c_arrive(h, a):
        for j in range(S):
            for d in range(1, C):
                c_copies[h, a, j, d].wait_recv()

    def weigh(h):
        own[h][0].wait()
        for d in range(1, G):
            z_copies[h, 0, d].wait_recv()
        c_arrive(h, 1)
        return soften(h)

    for h in range(hg):
        for a in (1, 2):
            own[h][a].wait()
            s_forward(h, a, 0)
    for w in weights:
        w.wait()
    for a in (1, 2):
        for h in range(hg):
            spread(h, (a,))
    for h in range(hg):
        pass_on(h, (1,))
    for h in range(1, hg):
        if h == 1:
            for i, d in enumerate(near):
                @pl.when(near_ok(d))
                def _():
                    m_copy(i, d).wait_recv()
            codes = jnp.concatenate([code[i, 0:1, 0:T] for i in range(n_near + 1)], axis=1)
            spots = jnp.concatenate(
                [
                    ((row - d) * C + col) * T + lax.broadcasted_iota(jnp.int32, (1, T), 1)
                    for d in [0] + near
                ],
                axis=1,
            )
            mine = (row * C + col) * T + sub
            same = codes == owner_col.astype(jnp.float32)
            gap_f = jnp.abs(mine // (GH * GW) - spots // (GH * GW))
            gap_h = jnp.abs(mine // GW % GH - spots // GW % GH)
            gap_w = jnp.abs(mine % GW - spots % GW)
            for j in range(RHEADS):
                ok = (
                    same
                    & (gap_f <= reach_ref[j, 0])
                    & (gap_h <= reach_ref[j, 1])
                    & (gap_w <= reach_ref[j, 2])
                )
                bias[j * T : (j + 1) * T] = jnp.where(ok, 0.0, NEG)
    last = hg - 1
    weighed = []
    for h in range(last):
        pass_on(h, (2,))
        weighed.append(weigh(h))
    pass_on(last, (2,))
    for h in range(last):
        c_arrive(h, 2)
        acc[...] = blend(h, *weighed[h])
    weighed.append(weigh(last))
    c_arrive(last, 2)
    share = blend(last, *weighed[last])
    part_out[...] = share.astype(jnp.bfloat16)
    p_copies = {}
    for d in range(1, G):
        to = lax.rem(g + d, G)
        p_copies[d] = pltpu.make_async_remote_copy(
            src_ref=part_out.at[to],
            dst_ref=part_in.at[d - 1],
            send_sem=p_send.at[d - 1],
            recv_sem=p_recv.at[d - 1],
            device_id=(grp, to * S + s, col),
            device_id_type=MESH,
        )
        p_copies[d].start()
    acc[...] = share
    velocity = acc[g]
    for d in range(1, G):
        p_copies[d].wait_recv()
        velocity = velocity + part_in[d - 1].astype(jnp.float32)
    updated = lat[...] + 0.5 * velocity
    fine = updated.astype(jnp.bfloat16)
    nb[0] = fine

    def n_copy(i, d):
        return pltpu.make_async_remote_copy(
            src_ref=nb.at[0],
            dst_ref=nb.at[i + 1],
            send_sem=n_send.at[i],
            recv_sem=n_recv.at[i],
            device_id=(grp, row + d, col),
            device_id_type=MESH,
        )

    for i, d in enumerate(near):
        @pl.when(goes(d))
        def _():
            n_copy(i, d).start()
    upd_ref[...] = 0.5 * velocity
    rquery = jnp.dot(fine, rw[0], preferred_element_type=jnp.float32).astype(jnp.bfloat16)
    rhead = LAT // RHEADS
    part_of = lax.broadcasted_iota(jnp.int32, (T, LAT), 1) // rhead
    stacked = jnp.concatenate(
        [jnp.where(part_of == j, rquery, jnp.zeros_like(rquery)) for j in range(RHEADS)], axis=0
    )
    for i, d in enumerate(near):
        @pl.when(near_ok(d))
        def _():
            n_copy(i, d).wait_recv()
    around = nb[...].reshape((n_near + 1) * T, LAT)
    rkey = jnp.dot(around, rw[1], preferred_element_type=jnp.float32).astype(jnp.bfloat16)
    rvalue = jnp.dot(around, rw[2], preferred_element_type=jnp.float32).astype(jnp.bfloat16)
    scores = lax.dot_general(
        stacked, rkey, (((1,), (1,)), ((), ())), preferred_element_type=jnp.float32
    )
    scores = scores * (1.0 / math.sqrt(rhead)) + bias[...]
    terms = jnp.exp(scores - jnp.max(scores, axis=1, keepdims=True))
    total = jnp.sum(terms, axis=1, keepdims=True)
    mixed = jnp.dot(terms.astype(jnp.bfloat16), rvalue, preferred_element_type=jnp.float32) / total
    joined = mixed[0:T]
    for j in range(1, RHEADS):
        joined = jnp.where(part_of == j, mixed[j * T : (j + 1) * T], joined)
    delta = jnp.dot(
        joined.astype(jnp.bfloat16), ro[...], preferred_element_type=jnp.float32
    ).astype(jnp.bfloat16)
    ref_ref[...] = jnp.where(live_col > 0, delta.astype(jnp.float32), 0.0)

    for copies in (z_copies, s_copies, c_copies, p_copies):
        for copy in copies.values():
            copy.wait_send()
    for i, d in enumerate(near):
        @pl.when(goes(d))
        def _():
            m_copy(i, d).wait_send()
            n_copy(i, d).wait_send()


def per_device(
    queries, key_rows, value_rows, latent, out_proj, tile_owner, tile_count, window_reach,
    refine_query, refine_key, refine_value, refine_out,
):
    R, C = lax.axis_size("row"), lax.axis_size("col")
    T = queries.shape[0]
    heads = queries.shape[1] // HEAD
    G = math.gcd(heads, R)
    S = R // G
    hg = heads // G
    near = near_rows(R, C, T)
    n = len(near)
    any_spec = pl.BlockSpec(memory_space=pl.ANY)
    smem = pl.BlockSpec(memory_space=pltpu.SMEM)
    vmem = pl.BlockSpec(memory_space=pltpu.VMEM)
    dma = pltpu.SemaphoreType.DMA
    bf16, f32 = jnp.bfloat16, jnp.float32
    half, delta = pl.pallas_call(
        functools.partial(kernel, (G, S, C, hg, T), near),
        out_shape=(
            jax.ShapeDtypeStruct((T, LAT), f32),
            jax.ShapeDtypeStruct((T, LAT), f32),
        ),
        in_specs=[any_spec] * 5 + [smem] * 3 + [any_spec] * 4,
        out_specs=(vmem, vmem),
        scratch_shapes=[
            pltpu.VMEM((hg, G, T, HEAD), bf16),
            pltpu.VMEM((hg, S, C, G, T, HEAD), bf16),
            pltpu.VMEM((hg, S, C, G, T, HEAD), bf16),
            pltpu.VMEM((hg * HEAD, LAT), bf16),
            pltpu.VMEM((T, LAT), f32),
            pltpu.VMEM((3, LAT, LAT), bf16),
            pltpu.VMEM((LAT, LAT), bf16),
            pltpu.VMEM((G, T, LAT), f32),
            pltpu.VMEM((G, T, LAT), bf16),
            pltpu.VMEM((G - 1, T, LAT), bf16),
            pltpu.VMEM((n + 1, T, LAT), bf16),
            pltpu.VMEM((n + 1, 8, 128), f32),
            pltpu.VMEM((RHEADS * T, (n + 1) * T), f32),
            dma((hg, 3, G - 1)),
            dma((hg, 3, G - 1)),
            dma((hg, 2, G, max(S - 1, 1))),
            dma((hg, 2, G, max(S - 1, 1))),
            dma((hg, 2, S, max(C - 1, 1))),
            dma((hg, 2, S, max(C - 1, 1))),
            dma((G - 1,)),
            dma((G - 1,)),
            dma((n,)),
            dma((n,)),
            dma((n,)),
            dma((n,)),
            dma((hg, 3)),
            dma((6,)),
        ],
        compiler_params=pltpu.CompilerParams(collective_id=0, has_side_effects=True),
    )(
        queries, key_rows, value_rows, latent, out_proj, tile_owner.reshape(-1), tile_count,
        window_reach, refine_query, refine_key, refine_value, refine_out,
    )
    updated = latent + half
    return updated, updated + delta


def solution(mesh):
    return jax.shard_map(
        per_device,
        mesh=mesh,
        in_specs=(
            P(("grp", "row", "col"), None),
            P(("grp", "row", "col"), None),
            P(("grp", "row", "col"), None),
            P(("grp", "row", "col"), None),
            P(),
            P(("grp", "row", "col"), None),
            P(("grp", "row", "col")),
            P(),
            P(),
            P(),
            P(),
            P(),
        ),
        out_specs=(P(("grp", "row", "col"), None), P(("grp", "row", "col"), None)),
        check_vma=False,
    )
```

profile of v0, /device:TPU:0, one launch (start us, length us, event | category | flops | bytes accessed | tf_op | source)
XLA Modules:
  0.0 34.4 jit_solution(10832335013834372261)
XLA Ops:
  0.6 0.0 copy-start
  0.6 32.3 %shard_map.131 = (f32[64,128]{1,0:T(8,128)}, f32[64,128]{1,0:T(8,128)}) custom-call(bf16[64,1536]{1,0:T(8,128)(2,1)} %q_hbm.1, bf16[64,1536]{1,0:T(8,128)(2,1)} %k_hbm.1, bf16[64,1536]{1,0:T(8,128)(2,1)} %v_hbm.1, f32[64,128]{1,0:T(8,128)} %lat_hbm.1, bf16[1536,128]{1,0:T(8,128)(2,1)} %wo_hbm.1, s32[16]{0:T(128)} %bitcast.1, s32[16]{0:T(128)} %count_ref.1, ...), custom_call_target="tpu_custom_call" | custom-call | tf_op jit(solution)/shard_map/pallas_call | solution.py:395
  33.0 0.0 copy-done
  33.0 1.4 %fusion = (f32[64,128]{1,0:T(8,128)}, f32[64,128]{1,0:T(8,128)}) fusion(f32[64,128]{1,0:T(8,128)} %get-tuple-element.5, f32[64,128]{1,0:T(8,128)S(1)} %copy-done, f32[64,128]{1,0:T(8,128)} %get-tuple-element.4), kind=kLoop, calls=%fused_computation | loop fusion | flops 16384 | bytes 163840 | tf_op jit(solution)/shard_map/add | solution.py:438
Async XLA Ops:
  0.6 32.3 %copy-start = (f32[64,128]{1,0:T(8,128)S(1)}, f32[64,128]{1,0:T(8,128)}, u32[]{:S(2)}) copy-start(f32[64,128]{1,0:T(8,128)} %lat_hbm.1) | copy-start | bytes 98308
where the time goes:
time: 34.6 us; the launch traced here: 34.4 us
  Pallas kernels  32.3 us (93%)
  other arithmetic  1.41 us (4%)
  between operations  0.66 us (2%)
    pallas_call x1, Pallas kernels, per_device(): pl.pallas_call(functools.partial(kernel, (G, S, C, hg, T), near), out_sha...  32.3 us
    add x1, other arithmetic, per_device(): return (updated, updated + delta)  1.41 us

commit v1 on v0

--- a/solution.py
+++ b/solution.py
@@ -42,12 +42,13 @@
 
 def kernel(
     dims, near,
-    q_hbm, k_hbm, v_hbm, lat_hbm, wo_hbm, owner_ref, count_ref, reach_ref,
+    q_hbm, k_hbm, v_hbm, lat_hbm, wo_hbm, owner_hbm, count_hbm, reach_hbm,
     rq_hbm, rk_hbm, rv_hbm, ro_hbm,
     upd_ref, ref_ref,
     qb, kb, vb, wo, lat, rw, ro, acc, part_out, part_in, nb, code, bias,
+    owner_ref, count_ref, reach_ref,
     z_send, z_recv, s_send, s_recv, c_send, c_recv, p_send, p_recv,
-    n_send, n_recv, m_send, m_recv, own_sem, w_sem,
+    n_send, n_recv, m_send, m_recv, own_sem, w_sem, i_sem,
 ):
     G, S, C, hg, T = dims
     R = G * S
@@ -88,6 +89,12 @@
         pltpu.make_async_copy(ro_hbm, ro, w_sem.at[5]),
     ]
 
+    tables = [
+        pltpu.make_async_copy(owner_hbm, owner_ref, i_sem.at[0]),
+        pltpu.make_async_copy(count_hbm, count_ref, i_sem.at[1]),
+        pltpu.make_async_copy(reach_hbm, reach_ref, i_sem.at[2]),
+    ]
+
     barrier = pltpu.get_barrier_semaphore()
     greeted = (
         [(lax.rem(g + d, G) * S + s, col) for d in range(1, G)]
@@ -104,11 +111,15 @@
                 barrier, inc=1, device_id=(grp, row + d, col), device_id_type=MESH
             )
 
+    for t in tables:
+        t.start()
     for h in range(hg):
         for a in range(3):
             own[h][a].start()
     for w in weights:
         w.start()
+    for t in tables:
+        t.wait()
 
     lane = lax.broadcasted_iota(jnp.int32, (8, 128), 1)
     sub = lax.broadcasted_iota(jnp.int32, (T, 1), 0)
@@ -388,17 +399,16 @@
     near = near_rows(R, C, T)
     n = len(near)
     any_spec = pl.BlockSpec(memory_space=pl.ANY)
-    smem = pl.BlockSpec(memory_space=pltpu.SMEM)
     vmem = pl.BlockSpec(memory_space=pltpu.VMEM)
     dma = pltpu.SemaphoreType.DMA
     bf16, f32 = jnp.bfloat16, jnp.float32
     half, delta = pl.pallas_call(
         functools.partial(kernel, (G, S, C, hg, T), near),
         out_shape=(
-            jax.ShapeDtypeStruct((T, LAT), f32),
-            jax.ShapeDtypeStruct((T, LAT), f32),
+            pltpu.VMEM((T, LAT), f32),
+            pltpu.VMEM((T, LAT), f32),
         ),
-        in_specs=[any_spec] * 5 + [smem] * 3 + [any_spec] * 4,
+        in_specs=[any_spec] * 12,
         out_specs=(vmem, vmem),
         scratch_shapes=[
             pltpu.VMEM((hg, G, T, HEAD), bf16),
@@ -414,6 +424,9 @@
             pltpu.VMEM((n + 1, T, LAT), bf16),
             pltpu.VMEM((n + 1, 8, 128), f32),
             pltpu.VMEM((RHEADS * T, (n + 1) * T), f32),
+            pltpu.SMEM((T // TILE,), jnp.int32),
+            pltpu.SMEM((T // TILE,), jnp.int32),
+            pltpu.SMEM((RHEADS, 3), jnp.int32),
             dma((hg, 3, G - 1)),
             dma((hg, 3, G - 1)),
             dma((hg, 2, G, max(S - 1, 1))),
@@ -428,6 +441,7 @@
             dma((n,)),
             dma((hg, 3)),
             dma((6,)),
+            dma((3,)),
         ],
         compiler_params=pltpu.CompilerParams(collective_id=0, has_side_effects=True),
     )(

time: 34.6 us -> 32.5 us (0.939)
  Pallas kernels: 32.3 us -> 31 us
  other arithmetic: 1.41 us -> 0.63 us
    pallas_call x1, Pallas kernels: 32.3 us -> 31 us  [per_device(): pl.pallas_call(functools.partial(kernel, (G, S, C, hg, T), near), out_sha...]
    add x1, other arithmetic: 1.41 us -> 0.63 us  [per_device(): return (updated, updated + delta)]
where the time goes in v1:
time: 32.5 us; the launch traced here: 32.3 us
  Pallas kernels  31 us (95%)
  between operations  0.66 us (2%)
  other arithmetic  0.63 us (2%)
    pallas_call x1, Pallas kernels, per_device(): pl.pallas_call(functools.partial(kernel, (G, S, C, hg, T), near), out_sha...  31 us

profile of v1, /device:TPU:0, one launch (start us, length us, event | category | flops | bytes accessed | tf_op | source)
XLA Modules:
  0.0 32.3 jit_solution(6962545707501948565)
XLA Ops:
  0.6 0.0 copy-start
  0.6 31.0 %shard_map.131 = (f32[64,128]{1,0:T(8,128)S(1)}, f32[64,128]{1,0:T(8,128)S(1)}) custom-call(bf16[64,1536]{1,0:T(8,128)(2,1)} %q_hbm.1, bf16[64,1536]{1,0:T(8,128)(2,1)} %k_hbm.1, bf16[64,1536]{1,0:T(8,128)(2,1)} %v_hbm.1, f32[64,128]{1,0:T(8,128)} %lat_hbm.1, bf16[1536,128]{1,0:T(8,128)(2,1)} %wo_hbm.1, s32[16]{0:T(128)} %bitcast.1, s32[16]{0:T(128)} %count_hbm.1, ...), custom_call_target="tpu_custom_call" | custom-call | tf_op jit(solution)/shard_map/pallas_call | solution.py:405
  31.7 0.0 copy-done
  31.7 0.6 %fusion = (f32[64,128]{1,0:T(8,128)}, f32[64,128]{1,0:T(8,128)}) fusion(f32[64,128]{1,0:T(8,128)S(1)} %get-tuple-element.5, f32[64,128]{1,0:T(8,128)S(1)} %copy-done, f32[64,128]{1,0:T(8,128)S(1)} %get-tuple-element.4), kind=kLoop, calls=%fused_computation | loop fusion | flops 16384 | bytes 163840 | tf_op jit(solution)/shard_map/add | solution.py:452
Async XLA Ops:
  0.6 31.0 %copy-start = (f32[64,128]{1,0:T(8,128)S(1)}, f32[64,128]{1,0:T(8,128)}, u32[]{:S(2)}) copy-start(f32[64,128]{1,0:T(8,128)} %lat_hbm.1) | copy-start | bytes 98308

commit v2 on v1

--- a/solution.py
+++ b/solution.py
@@ -151,22 +151,41 @@
         barrier, len(greeted) + sum([near_ok(d).astype(jnp.int32) for d in near])
     )
 
-    def z_copy(h, a, d):
-        to = lax.rem(g + d, G)
+    def far(k):
+        down = jnp.where(G - 1 - k > g, G - 1 - k, G - 2 - k)
+        return jnp.where(2 * g < G, down, jnp.where(k < g, k, k + 1))
+
+    def close(k):
+        return far(G - 2 - k)
+
+    def z_copy(h, a, to):
         return pltpu.make_async_remote_copy(
             src_ref=arrays[a][0].at[:, head_cols(to, h)],
             dst_ref=slot(a, h, g),
-            send_sem=z_send.at[h, a, d - 1],
-            recv_sem=z_recv.at[h, a, d - 1],
+            send_sem=z_send.at[h, a, to],
+            recv_sem=z_recv.at[h, a, g],
             device_id=(grp, to * S + s, col),
             device_id_type=MESH,
         )
 
     z_copies = {}
-    for h, a in [(h, a) for a in (1, 2, 0) for h in range(hg)]:
-        for d in list(range(2, G)) + [1]:
-            z_copies[h, a, d] = z_copy(h, a, d)
-            z_copies[h, a, d].start()
+    def z_start(kinds):
+        for h, a in [(h, a) for a in kinds for h in range(hg)]:
+            for k in range(G - 1):
+                z_copies[h, a, k] = z_copy(h, a, far(k))
+                z_copies[h, a, k].start()
+
+    def z_arrived(h, a, frm):
+        pltpu.make_async_remote_copy(
+            src_ref=slot(a, h, frm),
+            dst_ref=slot(a, h, frm),
+            send_sem=z_send.at[h, a, frm],
+            recv_sem=z_recv.at[h, a, frm],
+            device_id=(grp, frm * S + s, col),
+            device_id_type=MESH,
+        ).wait_recv()
+
+    z_start((1, 2))
 
     def m_copy(i, d):
         return pltpu.make_async_remote_copy(
@@ -199,15 +218,15 @@
             )
             c_copies[h, a, j, d].start()
 
-    def s_forward(h, a, e):
+    def s_forward(h, a, frm, e):
         buf = arrays[a][1]
-        block = buf.at[h, s, col, lax.rem(g - e + G, G)]
+        block = buf.at[h, s, col, frm]
         for d in range(1, S):
             s_copies[h, a, e, d] = pltpu.make_async_remote_copy(
                 src_ref=block,
                 dst_ref=block,
-                send_sem=s_send.at[h, a - 1, e, d - 1],
-                recv_sem=s_recv.at[h, a - 1, e, d - 1],
+                send_sem=s_send.at[h, a - 1, frm, d - 1],
+                recv_sem=s_recv.at[h, a - 1, frm, d - 1],
                 device_id=(grp, g * S + lax.rem(s + d, S), col),
                 device_id_type=MESH,
             )
@@ -215,9 +234,9 @@
 
     def spread(h, kinds=(1, 2)):
         for a in kinds:
-            for e in range(1, G):
-                z_copies[h, a, e].wait_recv()
-                s_forward(h, a, e)
+            for k in range(G - 1):
+                z_arrived(h, a, close(k))
+                s_forward(h, a, close(k), k + 1)
             c_forward(h, a, 0)
 
     def pass_on(h, kinds=(1, 2)):
@@ -256,20 +275,23 @@
 
     def weigh(h):
         own[h][0].wait()
-        for d in range(1, G):
-            z_copies[h, 0, d].wait_recv()
+        for k in range(G - 1):
+            z_arrived(h, 0, close(k))
         c_arrive(h, 1)
         return soften(h)
 
     for h in range(hg):
         for a in (1, 2):
             own[h][a].wait()
-            s_forward(h, a, 0)
+            s_forward(h, a, g, 0)
     for w in weights:
         w.wait()
-    for a in (1, 2):
-        for h in range(hg):
-            spread(h, (a,))
+    for h in range(hg):
+        spread(h, (1,))
+    for h in range(hg):
+        spread(h, (2,))
+        if h == 1:
+            z_start((0,))
     for h in range(hg):
         pass_on(h, (1,))
     for h in range(1, hg):
@@ -313,22 +335,30 @@
     share = blend(last, *weighed[last])
     part_out[...] = share.astype(jnp.bfloat16)
     p_copies = {}
-    for d in range(1, G):
-        to = lax.rem(g + d, G)
-        p_copies[d] = pltpu.make_async_remote_copy(
+    for k in range(G - 1):
+        to = far(k)
+        p_copies[k] = pltpu.make_async_remote_copy(
             src_ref=part_out.at[to],
-            dst_ref=part_in.at[d - 1],
-            send_sem=p_send.at[d - 1],
-            recv_sem=p_recv.at[d - 1],
+            dst_ref=part_in.at[g],
+            send_sem=p_send.at[to],
+            recv_sem=p_recv.at[g],
             device_id=(grp, to * S + s, col),
             device_id_type=MESH,
         )
-        p_copies[d].start()
+        p_copies[k].start()
     acc[...] = share
     velocity = acc[g]
-    for d in range(1, G):
-        p_copies[d].wait_recv()
-        velocity = velocity + part_in[d - 1].astype(jnp.float32)
+    for k in range(G - 1):
+        frm = close(k)
+        pltpu.make_async_remote_copy(
+            src_ref=part_in.at[frm],
+            dst_ref=part_in.at[frm],
+            send_sem=p_send.at[frm],
+            recv_sem=p_recv.at[frm],
+            device_id=(grp, frm * S + s, col),
+            device_id_type=MESH,
+        ).wait_recv()
+        velocity = velocity + part_in[frm].astype(jnp.float32)
     updated = lat[...] + 0.5 * velocity
     fine = updated.astype(jnp.bfloat16)
     nb[0] = fine
@@ -420,21 +450,21 @@
             pltpu.VMEM((LAT, LAT), bf16),
             pltpu.VMEM((G, T, LAT), f32),
             pltpu.VMEM((G, T, LAT), bf16),
-            pltpu.VMEM((G - 1, T, LAT), bf16),
+            pltpu.VMEM((G, T, LAT), bf16),
             pltpu.VMEM((n + 1, T, LAT), bf16),
             pltpu.VMEM((n + 1, 8, 128), f32),
             pltpu.VMEM((RHEADS * T, (n + 1) * T), f32),
             pltpu.SMEM((T // TILE,), jnp.int32),
             pltpu.SMEM((T // TILE,), jnp.int32),
             pltpu.SMEM((RHEADS, 3), jnp.int32),
-            dma((hg, 3, G - 1)),
-            dma((hg, 3, G - 1)),
+            dma((hg, 3, G)),
+            dma((hg, 3, G)),
             dma((hg, 2, G, max(S - 1, 1))),
             dma((hg, 2, G, max(S - 1, 1))),
             dma((hg, 2, S, max(C - 1, 1))),
             dma((hg, 2, S, max(C - 1, 1))),
-            dma((G - 1,)),
-            dma((G - 1,)),
+            dma((G,)),
+            dma((G,)),
             dma((n,)),
             dma((n,)),
             dma((n,)),

time: 32.5 us -> 31.7 us (0.975)
  Pallas kernels: 31 us -> 30.2 us
    pallas_call x1, Pallas kernels: 31 us -> 30.2 us  [per_device(): pl.pallas_call(functools.partial(kernel, (G, S, C, hg, T), near), out_sha...]
where the time goes in v2:
time: 31.7 us; the launch traced here: 31.5 us
  Pallas kernels  30.2 us (95%)
  between operations  0.66 us (2%)
  other arithmetic  0.63 us (2%)
    pallas_call x1, Pallas kernels, per_device(): pl.pallas_call(functools.partial(kernel, (G, S, C, hg, T), near), out_sha...  30.2 us
    add x1, other arithmetic, per_device(): return (updated, updated + delta)  0.63 us

profile of v2, /device:TPU:0, one launch (start us, length us, event | category | flops | bytes accessed | tf_op | source)
XLA Modules:
  0.0 31.5 jit_solution(1661634813042137673)
XLA Ops:
  0.6 0.0 copy-start
  0.6 30.2 %shard_map.131 = (f32[64,128]{1,0:T(8,128)S(1)}, f32[64,128]{1,0:T(8,128)S(1)}) custom-call(bf16[64,1536]{1,0:T(8,128)(2,1)} %q_hbm.1, bf16[64,1536]{1,0:T(8,128)(2,1)} %k_hbm.1, bf16[64,1536]{1,0:T(8,128)(2,1)} %v_hbm.1, f32[64,128]{1,0:T(8,128)} %lat_hbm.1, bf16[1536,128]{1,0:T(8,128)(2,1)} %wo_hbm.1, s32[16]{0:T(128)} %bitcast.1, s32[16]{0:T(128)} %count_hbm.1, ...), custom_call_target="tpu_custom_call" | custom-call | tf_op jit(solution)/shard_map/pallas_call | solution.py:435
  30.9 0.0 copy-done
  30.9 0.6 %fusion = (f32[64,128]{1,0:T(8,128)}, f32[64,128]{1,0:T(8,128)}) fusion(f32[64,128]{1,0:T(8,128)S(1)} %get-tuple-element.5, f32[64,128]{1,0:T(8,128)S(1)} %copy-done, f32[64,128]{1,0:T(8,128)S(1)} %get-tuple-element.4), kind=kLoop, calls=%fused_computation | loop fusion | flops 16384 | bytes 163840 | tf_op jit(solution)/shard_map/add | solution.py:482
Async XLA Ops:
  0.6 30.3 %copy-start = (f32[64,128]{1,0:T(8,128)S(1)}, f32[64,128]{1,0:T(8,128)}, u32[]{:S(2)}) copy-start(f32[64,128]{1,0:T(8,128)} %lat_hbm.1) | copy-start | bytes 98308

commit v3 on v2

--- a/solution.py
+++ b/solution.py
@@ -262,23 +262,18 @@
     def blend(h, terms, total):
         value = vb[h].reshape(keys, HEAD)
         mixed = jnp.dot(terms, value, preferred_element_type=jnp.float32)
-        attended = (mixed / total).astype(jnp.bfloat16)
-        share = jnp.dot(
-            attended, wo[h * HEAD : (h + 1) * HEAD], preferred_element_type=jnp.float32
-        ).reshape(G, T, LAT)
-        return share if h == 0 else acc[...] + share
+        return (mixed / total).astype(jnp.bfloat16)
 
     def c_arrive(h, a):
         for j in range(S):
             for d in range(1, C):
                 c_copies[h, a, j, d].wait_recv()
 
-    def weigh(h):
+    def ready(h):
         own[h][0].wait()
         for k in range(G - 1):
             z_arrived(h, 0, close(k))
         c_arrive(h, 1)
-        return soften(h)
 
     for h in range(hg):
         for a in (1, 2):
@@ -294,45 +289,23 @@
             z_start((0,))
     for h in range(hg):
         pass_on(h, (1,))
-    for h in range(1, hg):
-        if h == 1:
-            for i, d in enumerate(near):
-                @pl.when(near_ok(d))
-                def _():
-                    m_copy(i, d).wait_recv()
-            codes = jnp.concatenate([code[i, 0:1, 0:T] for i in range(n_near + 1)], axis=1)
-            spots = jnp.concatenate(
-                [
-                    ((row - d) * C + col) * T + lax.broadcasted_iota(jnp.int32, (1, T), 1)
-                    for d in [0] + near
-                ],
-                axis=1,
-            )
-            mine = (row * C + col) * T + sub
-            same = codes == owner_col.astype(jnp.float32)
-            gap_f = jnp.abs(mine // (GH * GW) - spots // (GH * GW))
-            gap_h = jnp.abs(mine // GW % GH - spots // GW % GH)
-            gap_w = jnp.abs(mine % GW - spots % GW)
-            for j in range(RHEADS):
-                ok = (
-                    same
-                    & (gap_f <= reach_ref[j, 0])
-                    & (gap_h <= reach_ref[j, 1])
-                    & (gap_w <= reach_ref[j, 2])
-                )
-                bias[j * T : (j + 1) * T] = jnp.where(ok, 0.0, NEG)
     last = hg - 1
     weighed = []
     for h in range(last):
         pass_on(h, (2,))
-        weighed.append(weigh(h))
+        if h > 0:
+            for e in range(last):
+                ready(e)
+            weighed = [soften(e) for e in range(last)]
     pass_on(last, (2,))
-    for h in range(last):
+    for h in range(hg):
         c_arrive(h, 2)
-        acc[...] = blend(h, *weighed[h])
-    weighed.append(weigh(last))
-    c_arrive(last, 2)
-    share = blend(last, *weighed[last])
+    ready(last)
+    weighed.append(soften(last))
+    share = jnp.dot(
+        jnp.concatenate([blend(h, *weighed[h]) for h in range(hg)], axis=1), wo[...],
+        preferred_element_type=jnp.float32,
+    ).reshape(G, T, LAT)
     part_out[...] = share.astype(jnp.bfloat16)
     p_copies = {}
     for k in range(G - 1):
@@ -348,6 +321,31 @@
         p_copies[k].start()
     acc[...] = share
     velocity = acc[g]
+    for i, d in enumerate(near):
+        @pl.when(near_ok(d))
+        def _():
+            m_copy(i, d).wait_recv()
+    codes = jnp.concatenate([code[i, 0:1, 0:T] for i in range(n_near + 1)], axis=1)
+    spots = jnp.concatenate(
+        [
+            ((row - d) * C + col) * T + lax.broadcasted_iota(jnp.int32, (1, T), 1)
+            for d in [0] + near
+        ],
+        axis=1,
+    )
+    mine = (row * C + col) * T + sub
+    same = codes == owner_col.astype(jnp.float32)
+    gap_f = jnp.abs(mine // (GH * GW) - spots // (GH * GW))
+    gap_h = jnp.abs(mine // GW % GH - spots // GW % GH)
+    gap_w = jnp.abs(mine % GW - spots % GW)
+    for j in range(RHEADS):
+        ok = (
+            same
+            & (gap_f <= reach_ref[j, 0])
+            & (gap_h <= reach_ref[j, 1])
+            & (gap_w <= reach_ref[j, 2])
+        )
+        bias[j * T : (j + 1) * T] = jnp.where(ok, 0.0, NEG)
     for k in range(G - 1):
         frm = close(k)
         pltpu.make_async_remote_copy(

time: 31.7 us -> 31.1 us (0.981)
  Pallas kernels: 30.2 us -> 29.7 us
    pallas_call x1, Pallas kernels: 30.2 us -> 29.7 us  [per_device(): pl.pallas_call(functools.partial(kernel, (G, S, C, hg, T), near), out_sha...]
where the time goes in v3:
time: 31.1 us; the launch traced here: 31 us
  Pallas kernels  29.7 us (95%)
  between operations  0.66 us (2%)
  other arithmetic  0.63 us (2%)
    pallas_call x1, Pallas kernels, per_device(): pl.pallas_call(functools.partial(kernel, (G, S, C, hg, T), near), out_sha...  29.7 us
    add x1, other arithmetic, per_device(): return (updated, updated + delta)  0.63 us

profile of v3, /device:TPU:0, one launch (start us, length us, event | category | flops | bytes accessed | tf_op | source)
XLA Modules:
  0.0 31.0 jit_solution(10868698724388007203)
XLA Ops:
  0.6 0.0 copy-start
  0.6 29.7 %shard_map.131 = (f32[64,128]{1,0:T(8,128)S(1)}, f32[64,128]{1,0:T(8,128)S(1)}) custom-call(bf16[64,1536]{1,0:T(8,128)(2,1)} %q_hbm.1, bf16[64,1536]{1,0:T(8,128)(2,1)} %k_hbm.1, bf16[64,1536]{1,0:T(8,128)(2,1)} %v_hbm.1, f32[64,128]{1,0:T(8,128)} %lat_hbm.1, bf16[1536,128]{1,0:T(8,128)(2,1)} %wo_hbm.1, s32[16]{0:T(128)} %bitcast.1, s32[16]{0:T(128)} %count_hbm.1, ...), custom_call_target="tpu_custom_call" | custom-call | tf_op jit(solution)/shard_map/pallas_call | solution.py:433
  30.3 0.0 copy-done
  30.3 0.6 %fusion = (f32[64,128]{1,0:T(8,128)}, f32[64,128]{1,0:T(8,128)}) fusion(f32[64,128]{1,0:T(8,128)S(1)} %get-tuple-element.5, f32[64,128]{1,0:T(8,128)S(1)} %copy-done, f32[64,128]{1,0:T(8,128)S(1)} %get-tuple-element.4), kind=kLoop, calls=%fused_computation | loop fusion | flops 16384 | bytes 163840 | tf_op jit(solution)/shard_map/add | solution.py:480
Async XLA Ops:
  0.6 29.7 %copy-start = (f32[64,128]{1,0:T(8,128)S(1)}, f32[64,128]{1,0:T(8,128)}, u32[]{:S(2)}) copy-start(f32[64,128]{1,0:T(8,128)} %lat_hbm.1) | copy-start | bytes 98308

commit v4 on v3

--- a/solution.py
+++ b/solution.py
@@ -45,7 +45,7 @@
     q_hbm, k_hbm, v_hbm, lat_hbm, wo_hbm, owner_hbm, count_hbm, reach_hbm,
     rq_hbm, rk_hbm, rv_hbm, ro_hbm,
     upd_ref, ref_ref,
-    qb, kb, vb, wo, lat, rw, ro, acc, part_out, part_in, nb, code, bias,
+    qb, kb, vb, wo, lat, rw, ro, fused, acc, part_out, part_in, nb, code, bias,
     owner_ref, count_ref, reach_ref,
     z_send, z_recv, s_send, s_recv, c_send, c_recv, p_send, p_recv,
     n_send, n_recv, m_send, m_recv, own_sem, w_sem, i_sem,
@@ -281,6 +281,14 @@
             s_forward(h, a, g, 0)
     for w in weights:
         w.wait()
+    rhead = LAT // RHEADS
+    part_of = lax.broadcasted_iota(jnp.int32, (T, LAT), 1) // rhead
+    column_of = lax.broadcasted_iota(jnp.int32, (LAT, LAT), 1) // rhead
+    for j in range(RHEADS):
+        value_part = jnp.where(column_of == j, rw[2], jnp.zeros_like(rw[2]))
+        fused[j * LAT : (j + 1) * LAT] = jnp.dot(
+            value_part, ro[...], preferred_element_type=jnp.float32
+        ).astype(jnp.bfloat16)
     for h in range(hg):
         spread(h, (1,))
     for h in range(hg):
@@ -377,31 +385,27 @@
             n_copy(i, d).start()
     upd_ref[...] = 0.5 * velocity
     rquery = jnp.dot(fine, rw[0], preferred_element_type=jnp.float32).astype(jnp.bfloat16)
-    rhead = LAT // RHEADS
-    part_of = lax.broadcasted_iota(jnp.int32, (T, LAT), 1) // rhead
     stacked = jnp.concatenate(
         [jnp.where(part_of == j, rquery, jnp.zeros_like(rquery)) for j in range(RHEADS)], axis=0
     )
+    probe = lax.dot_general(
+        stacked, rw[1], (((1,), (1,)), ((), ())), preferred_element_type=jnp.float32
+    ).astype(jnp.bfloat16)
     for i, d in enumerate(near):
         @pl.when(near_ok(d))
         def _():
             n_copy(i, d).wait_recv()
     around = nb[...].reshape((n_near + 1) * T, LAT)
-    rkey = jnp.dot(around, rw[1], preferred_element_type=jnp.float32).astype(jnp.bfloat16)
-    rvalue = jnp.dot(around, rw[2], preferred_element_type=jnp.float32).astype(jnp.bfloat16)
     scores = lax.dot_general(
-        stacked, rkey, (((1,), (1,)), ((), ())), preferred_element_type=jnp.float32
+        probe, around, (((1,), (1,)), ((), ())), preferred_element_type=jnp.float32
     )
     scores = scores * (1.0 / math.sqrt(rhead)) + bias[...]
     terms = jnp.exp(scores - jnp.max(scores, axis=1, keepdims=True))
     total = jnp.sum(terms, axis=1, keepdims=True)
-    mixed = jnp.dot(terms.astype(jnp.bfloat16), rvalue, preferred_element_type=jnp.float32) / total
-    joined = mixed[0:T]
-    for j in range(1, RHEADS):
-        joined = jnp.where(part_of == j, mixed[j * T : (j + 1) * T], joined)
-    delta = jnp.dot(
-        joined.astype(jnp.bfloat16), ro[...], preferred_element_type=jnp.float32
-    ).astype(jnp.bfloat16)
+    mixed = jnp.dot(terms.astype(jnp.bfloat16), around, preferred_element_type=jnp.float32)
+    mixed = (mixed / total).astype(jnp.bfloat16)
+    joined = jnp.concatenate([mixed[j * T : (j + 1) * T] for j in range(RHEADS)], axis=1)
+    delta = jnp.dot(joined, fused[...], preferred_element_type=jnp.float32).astype(jnp.bfloat16)
     ref_ref[...] = jnp.where(live_col > 0, delta.astype(jnp.float32), 0.0)
 
     for copies in (z_copies, s_copies, c_copies, p_copies):
@@ -446,6 +450,7 @@
             pltpu.VMEM((T, LAT), f32),
             pltpu.VMEM((3, LAT, LAT), bf16),
             pltpu.VMEM((LAT, LAT), bf16),
+            pltpu.VMEM((RHEADS * LAT, LAT), bf16),
             pltpu.VMEM((G, T, LAT), f32),
             pltpu.VMEM((G, T, LAT), bf16),
             pltpu.VMEM((G, T, LAT), bf16),

time: 31.1 us -> 31 us (level)
  no operation moved by 1% of the time
where the time goes in v4:
time: 31 us; the launch traced here: 30.8 us
  Pallas kernels  29.5 us (95%)
  between operations  0.66 us (2%)
  other arithmetic  0.63 us (2%)
    pallas_call x1, Pallas kernels, per_device(): pl.pallas_call(functools.partial(kernel, (G, S, C, hg, T), near), out_sha...  29.5 us
    add x1, other arithmetic, per_device(): return (updated, updated + delta)  0.63 us

profile of v4, /device:TPU:0, one launch (start us, length us, event | category | flops | bytes accessed | tf_op | source)
XLA Modules:
  0.0 30.8 jit_solution(10861930632190576229)
XLA Ops:
  0.6 0.0 copy-start
  0.6 29.5 %shard_map.131 = (f32[64,128]{1,0:T(8,128)S(1)}, f32[64,128]{1,0:T(8,128)S(1)}) custom-call(bf16[64,1536]{1,0:T(8,128)(2,1)} %q_hbm.1, bf16[64,1536]{1,0:T(8,128)(2,1)} %k_hbm.1, bf16[64,1536]{1,0:T(8,128)(2,1)} %v_hbm.1, f32[64,128]{1,0:T(8,128)} %lat_hbm.1, bf16[1536,128]{1,0:T(8,128)(2,1)} %wo_hbm.1, s32[16]{0:T(128)} %bitcast.1, s32[16]{0:T(128)} %count_hbm.1, ...), custom_call_target="tpu_custom_call" | custom-call | tf_op jit(solution)/shard_map/pallas_call | solution.py:437
  30.2 0.0 copy-done
  30.2 0.6 %fusion = (f32[64,128]{1,0:T(8,128)}, f32[64,128]{1,0:T(8,128)}) fusion(f32[64,128]{1,0:T(8,128)S(1)} %get-tuple-element.5, f32[64,128]{1,0:T(8,128)S(1)} %copy-done, f32[64,128]{1,0:T(8,128)S(1)} %get-tuple-element.4), kind=kLoop, calls=%fused_computation | loop fusion | flops 16384 | bytes 163840 | tf_op jit(solution)/shard_map/add | solution.py:485
Async XLA Ops:
  0.6 29.5 %copy-start = (f32[64,128]{1,0:T(8,128)S(1)}, f32[64,128]{1,0:T(8,128)}, u32[]{:S(2)}) copy-start(f32[64,128]{1,0:T(8,128)} %lat_hbm.1) | copy-start | bytes 98308
